TPU v7x, 256 devices: a whole 4x4x8 slice. The times are simulated.
256 devices in a mesh: scene: 128 (over x_lo, y, z, core), tile: 2 (over x_hi).
Axes of the slice: x: 4 (x_hi: 2, x_lo: 2; x = x_hi * 2 + x_lo), y: 4, z: 8, core: 2. Of those that a mesh axis runs over, the one named last changes fastest.
Arguments:
- features_in: bfloat16 [128, 4, 64, 4096], P('scene', 'tile'), may hold values from -6 to 6
- strided_weights: bfloat16 [2, 64, 1024], replicated, may hold values from -0.1875 to 0.1875
- dilated_weights: bfloat16 [2, 64, 576], replicated, may hold values from -0.25 to 0.25
- tile_bias: float32 [256, 64], replicated, may hold values from -3 to 3
- cost_cotangent: bfloat16 [128, 4, 1024], P('scene', 'tile'), may hold values from -6 to 6
- footprint_pairing: int32 [64, 4], replicated, may hold values from 0 to 3, each once within a row
- valid_counts: int32 [64], replicated, may hold values from 1 to 4, as said below
- tile_owner: int32 [128], replicated, may hold values from 0 to 255, as said below
Outputs:
- grad_features: bfloat16 [128, 4, 64, 4096], P('scene', 'tile')
- grad_weights: float32 [128, 1600], P('scene')
- grad_bias: float32 [256, 64], P(('scene', 'tile'))
Inputs may be any that keep to these rules, and one draw needn't show every extreme that they name: `footprint_pairing`: row k maps each patch of scene 2k to the patch of scene 2k + 1 that covers its footprint; each row is a permutation. `valid_counts`: patches 0 to count - 1 of both scenes of a pair are live; some pair has all 4 live. `tile_owner`: several scenes may share a tile, and many tiles have no scene.
All inputs are finite; a program needn't handle non-finite values.
Results may differ from a plain program's by a relative error of at most 0.007.
Values may be sent and summed in bfloat16 or wider, within the bound.
A program may use at most 64 MiB of HBM per device.

v0:
```python
import math
import jax
import jax.numpy as jnp
from jax import lax
from jax.sharding import PartitionSpec as P


def from_partner(x, axis, distance):
    return lax.ppermute(x, axis, [(i, i ^ 1 << distance) for i in range(lax.axis_size(axis))])


def apply_convolution(
    left_operand,
    right_operand,
    window_strides,
    border_padding,
    left_dilation,
    right_dilation,
    dimension_labels,
):
    return lax.conv_general_dilated(
        left_operand,
        right_operand,
        window_strides,
        border_padding,
        lhs_dilation=left_dilation,
        rhs_dilation=right_dilation,
        dimension_numbers=dimension_labels,
        preferred_element_type=jnp.float32,
    )


def silu_slope(pre_act):
    sigmoid_gate = jax.nn.sigmoid(pre_act)
    return sigmoid_gate * (1.0 + pre_act * (1.0 - sigmoid_gate))


def match_rows(pairing_row, branch, first_patch, patch_count):
    total_patches = pairing_row.shape[0]
    all_patches = jnp.arange(total_patches, dtype=jnp.int32)
    inverse = jnp.sum(
        jnp.where(pairing_row[:, None] == all_patches[None, :], all_patches[:, None], 0), axis=0
    )
    positions = first_patch + jnp.arange(patch_count, dtype=jnp.int32)
    return jnp.where(branch == 0, jnp.take(pairing_row, positions), jnp.take(inverse, positions))


def local(
    features_in,
    strided_weights,
    dilated_weights,
    tile_bias,
    cost_cotangent,
    footprint_pairing,
    valid_counts,
    tile_owner,
):
    scene_index = lax.axis_index("scene")
    tile_index = lax.axis_index("tile")
    branch = scene_index % 2
    pair_index = scene_index // 2
    features = features_in[0]
    own_cotangent = cost_cotangent[0]
    patches, channels, cells_in = (features.shape[0], features.shape[1], features.shape[2])
    cells_out = own_cotangent.shape[1]
    grid_side = math.isqrt(cells_in)
    half_side = grid_side // 2
    strided_kernel = lax.dynamic_index_in_dim(strided_weights, branch, 0, keepdims=False).reshape(
        channels, channels, 4, 4
    )
    dilated_kernel = lax.dynamic_index_in_dim(dilated_weights, branch, 0, keepdims=False).reshape(
        channels, channels, 3, 3
    )
    tile_id = lax.dynamic_index_in_dim(tile_owner, scene_index, 0, keepdims=False)
    bias_row = lax.dynamic_index_in_dim(tile_bias, tile_id, 0, keepdims=False)
    plain = ("NCHW", "OIHW", "NCHW")
    flipped = ("NCHW", "IOHW", "NCHW")
    kernel_side = ("CNHW", "IOHW", "CNHW")
    feature_grid = features.reshape(patches, channels, grid_side, grid_side)
    pre_act = (
        apply_convolution(
            feature_grid, strided_kernel, (2, 2), ((1, 1), (1, 1)), (1, 1), (1, 1), plain
        )
        + bias_row[None, :, None, None]
    )
    activation = jax.nn.silu(pre_act).astype(jnp.bfloat16)
    branch_grid = apply_convolution(
        activation, dilated_kernel, (1, 1), ((2, 2), (2, 2)), (1, 1), (2, 2), plain
    ).astype(jnp.bfloat16)
    branch_out = branch_grid.reshape(patches, channels, cells_out)
    pairing_row = lax.dynamic_index_in_dim(footprint_pairing, pair_index, 0, keepdims=False)
    first_patch = tile_index * patches
    swapped_out, swapped_cot = from_partner((branch_out, own_cotangent), "scene", 0)
    partner_out, partner_cot = (
        lax.all_gather(swapped_out, "tile", axis=0, tiled=True),
        lax.all_gather(swapped_cot, "tile", axis=0, tiled=True),
    )
    matched = match_rows(pairing_row, branch, first_patch, patches)
    chosen_out = jnp.take(partner_out, matched, axis=0)
    chosen_cot = jnp.take(partner_cot, matched, axis=0)
    pair_valid = lax.dynamic_index_in_dim(valid_counts, pair_index, 0, keepdims=False)
    live_count = jnp.clip(pair_valid - first_patch, 0, patches)
    live_mask = (jnp.arange(patches, dtype=jnp.int32) < live_count).astype(jnp.float32)
    signal = (own_cotangent.astype(jnp.float32) + chosen_cot.astype(jnp.float32)) * live_mask[
        :, None
    ]
    out_grad = (signal[:, None, :] * chosen_out.astype(jnp.float32)).astype(jnp.bfloat16)
    out_grid = out_grad.reshape(patches, channels, half_side, half_side)
    act_grad = apply_convolution(
        out_grid,
        dilated_kernel[:, :, ::-1, ::-1],
        (1, 1),
        ((2, 2), (2, 2)),
        (1, 1),
        (2, 2),
        flipped,
    )
    grad_dilated = apply_convolution(
        activation, out_grid, (2, 2), ((2, 2), (2, 2)), (1, 1), (1, 1), kernel_side
    )
    pre_grad = act_grad * silu_slope(pre_act)
    bias_grad = jnp.sum(pre_grad, axis=(0, 2, 3))
    pre_narrow = pre_grad.astype(jnp.bfloat16)
    grad_strided = apply_convolution(
        feature_grid, pre_narrow, (1, 1), ((1, 1), (1, 1)), (1, 1), (2, 2), kernel_side
    )
    feature_grad = apply_convolution(
        pre_narrow,
        strided_kernel[:, :, ::-1, ::-1],
        (1, 1),
        ((2, 2), (2, 2)),
        (2, 2),
        (1, 1),
        flipped,
    )
    feature_grads = feature_grad.astype(jnp.bfloat16).reshape(patches, channels, cells_in)
    grad_row = jnp.concatenate(
        [
            grad_strided.reshape(channels, 16 * channels),
            grad_dilated.reshape(channels, 9 * channels),
        ],
        axis=1,
    )
    scenes = lax.axis_size("scene")
    tile_devices = lax.axis_size("tile")
    weight_scale = 1.0 / math.sqrt(scenes * patches * tile_devices * cells_out)
    bias_scale = 1.0 / math.sqrt(patches * tile_devices * cells_out)
    branch_hit = jnp.arange(2, dtype=jnp.int32)[:, None, None] == branch
    weight_term = jnp.where(branch_hit, (grad_row * weight_scale)[None], jnp.float32(0.0)).reshape(
        2 * channels, 25 * channels
    )
    rows_each = 2 * channels // scenes
    summed = lax.psum(weight_term, ("scene", "tile"))
    grad_weights = lax.dynamic_slice_in_dim(summed, scene_index * rows_each, rows_each, 0)
    bias_rows = tile_bias.shape[0] // (scenes * tile_devices)
    scaled_bias = bias_grad * bias_scale
    owned_mask = tile_id == jnp.arange(
        lax.axis_size(("scene", "tile")) * bias_rows, dtype=jnp.int32
    )
    grad_bias = lax.psum_scatter(
        jnp.where(owned_mask[:, None], scaled_bias[None, :], jnp.float32(0.0)),
        ("scene", "tile"),
        scatter_dimension=0,
        tiled=True,
    )
    return (feature_grads[None], grad_weights, grad_bias)


def solution(mesh):
    return jax.shard_map(
        local,
        mesh=mesh,
        in_specs=(
            P("scene", "tile", None, None),
            P(),
            P(),
            P(),
            P("scene", "tile", None),
            P(),
            P(),
            P(),
        ),
        out_specs=(P("scene", "tile", None, None), P("scene", None), P(("scene", "tile"), None)),
        check_vma=False,
    )
```

profile of v0, /device:TPU:2, one launch (start us, length us, event | category | flops | bytes accessed | tf_op | source)
XLA Modules:
  0.0 381.2 jit_solution(3628517353644582072)
XLA Ops:
  7.4 1.3 dynamic_slice.30
  10.0 0.9 constant_dynamic-slice_fusion.1
  11.2 0.8 copy.171
  12.2 1.0 copy.169
  13.2 2.3 reshape_squeeze.3
  15.4 2.9 copy.200
  18.3 3.4 fusion.59
  21.8 2.7 fusion.12
  24.5 6.3 %copy.167 = bf16[64,64,2,8,13]{0,3,2,4,1:T(8,128)(2,1)} copy(bf16[64,64,2,8,13]{1,0,4,3,2:T(8,128)(2,1)} %fusion.12) | data formatting | bytes 3407872 | tf_op jit(solution)/shard_map/conv_general_dilated | solution.py:21
  31.4 0.2 dynamic-slice_reduce_fusion
  31.6 4.8 %fusion.27 = f32[32,16,5,64]{3,1,2,0:T(8,128)S(1)} fusion(bf16[64,64,4,4]{1,0,3,2:T(8,128)(2,1)S(1)} %copy-done.11, bf16[64,64,2,8,13]{0,3,2,4,1:T(8,128)(2,1)} %copy.167, f32[64]{0:T(128)S(1)} %dynamic-slice_reduce_fusion, pred[16,5]{0,1:T(8,128)(4,1)S(1)} %copy-done.17), kind=kOutput, calls=%fused_computation.39 | convolution fusion | flops 330629120 | bytes 2490704 | tf_op jit(solution)/shard_map/conv_general_dilated | solution.py:21
  36.5 0.5 select_bitcast_fusion
  37.1 0.5 copy-done.13
  37.5 1.7 convolution_convert_fusion.1
  39.2 0.2 copy.172
  39.5 1.0 copy.173
  40.5 0.4 collective-permute-start.1
  40.8 1.2 iota_compare_fusion.9
  42.0 0.8 fusion.58
  42.8 3.6 fusion.57
  46.4 0.6 dynamic_slice.28
  47.6 0.2 dynamic-slice_reduce_fusion.1
  47.9 0.6 gather_fusion.2
  48.6 0.6 gather_fusion.3
  49.2 4.2 %fusion.15 = (bf16[64,64,2,8,10]{1,0,4,3,2:T(8,128)(2,1)}, bf16[64,64,2,8,10]{1,0,4,3,2:T(8,128)(2,1)S(1)}) fusion(bf16[64,64,2,7,1]{1,0,4,3,2:T(8,128)(2,1)} %get-tuple-element.12, bf16[64,64,2,8,9]{1,0,4,3,2:T(8,128)(2,1)} %get-tuple-element.10, bf16[64,64,2,7,1]{1,0,4,3,2:T(8,128)(2,1)} %get-tuple-element.14, bf16[64,64,2,8,9]{1,0,4,3,2:T(8,128)(2,1)} %get-tuple-element.11), kind=kLoop, calls=%fused_computation.22 | loop fusion | flops 7864320 | bytes 5210112 | tf_op jit(solution)/shard_map/reshape;squeeze | solution.py:79
  53.4 0.7 slice.38
  54.2 0.9 copy-done.2
  55.1 2.3 fusion.17
  57.5 4.6 %copy.187 = bf16[64,64,2,8,10]{0,3,2,4,1:T(8,128)(2,1)} copy(bf16[64,64,2,8,10]{1,0,4,3,2:T(8,128)(2,1)} %copy-done.2) | data formatting | bytes 2621440 | tf_op jit(solution)/shard_map/reshape;squeeze | solution.py:79
  62.2 0.6 broadcast_in_dim.101
  63.0 2.9 copy.189
  66.0 4.8 %copy.185 = bf16[64,64,2,8,10]{0,3,2,4,1:T(8,128)(2,1)} copy(bf16[64,64,2,8,10]{1,0,4,3,2:T(8,128)(2,1)} %get-tuple-element.23) | data formatting | bytes 2621440 | tf_op jit(solution)/shard_map/reshape;squeeze | solution.py:79
  70.8 2.9 copy.188
  73.7 5.9 %all-gather = bf16[2,2,1024]{2,1,0:T(2,128)(2,1)S(1)} all-gather(bf16[1,2,1024]{2,1,0:T(2,128)(2,1)S(1)} %bitcast.88), channel_id=1, replica_groups=mesh['scene'=128,'tile'=2] {'tile'}, dimensions={0}, use_global_device_ids=true | all-gather | bytes 12288 | tf_op jit(solution)/shard_map/all_gather | solution.py:96
  79.6 0.6 gather_fusion
  80.3 1.2 copy.174
  81.6 9.4 %all_gather.7 = bf16[4,64,1024]{2,1,0:T(8,128)(2,1)S(1)} all-gather(bf16[2,64,1024]{2,1,0:T(8,128)(2,1)S(1)} %copy.174), channel_id=1, replica_groups=mesh['scene'=128,'tile'=2] {'tile'}, dimensions={0}, use_global_device_ids=true | all-gather | bytes 786432 | tf_op jit(solution)/shard_map/all_gather | solution.py:95
  90.9 0.6 gather_fusion.1
  91.5 0.3 copy.175
  91.8 0.3 fusion.66
  92.1 0.3 multiply_convert_fusion.1
  92.5 0.2 copy.201
  92.7 3.1 fusion.49
  95.8 0.2 copy.195
  96.5 0.2 fusion.30
  96.7 0.7 copy-done.9
  97.5 1.5 convert_select_fusion
  98.9 0.4 select_reduce_fusion
  99.6 0.4 copy-done.6
  100.0 0.8 copy-done.7
  100.8 1.0 copy-done.4
  101.7 5.0 %fusion = f32[64,64,4,4,1]{0,1,3,4,2:T(8,128)S(1)} fusion(bf16[64,64,16,10,1]{0,2,4,3,1:T(8,128)(2,1)S(1)} %bitcast.81, bf16[64,64,16,10,1]{0,2,4,3,1:T(8,128)(2,1)S(1)} %bitcast.79, bf16[64,64,16,10,1]{0,2,4,3,1:T(8,128)(2,1)S(1)} %copy-done.5, bf16[64,64,16,10,1]{0,2,4,3,1:T(8,128)(2,1)S(1)} %bitcast.80, bf16[32,16,5,64]{3,1,2,0:T(8,128)(2,1)S(1)} %get-tuple-element.21), kind=kOutput, calls=%fused_computation.4 | convolution fusion | flops 351272960 | bytes 5832704 | tf_op jit(solution)/shard_map/conv_general_dilated | solution.py:21
  106.7 0.3 copy.191
  107.1 0.2 copy.196
  107.3 0.7 broadcast_select_fusion
  108.0 0.2 fusion.43
  108.3 1.1 bitcast_select_fusion
  109.4 3.1 convolution_convert_fusion
  112.5 0.5 copy.182
  113.0 2.9 copy.183
  116.0 4.1 %broadcast_in_dim_reshape.3 = bf16[1,2,64,4096]{3,2,1,0:T(8,128)(2,1)} reshape(bf16[2,64,64,64]{3,2,1,0:T(8,128)(2,1)} %copy.183) | data formatting | bytes 2097152 | tf_op jit(solution)/shard_map/broadcast_in_dim;reshape | solution.py:166
  120.1 251.6 %all-reduce.4.cloned.1.call-done = (f32[128,1600]{1,0:T(8,128)}, f32[256,64]{1,0:T(8,128)}) async-done(((f32[128,1600]{1,0:T(8,128)}, f32[256,64]{1,0:T(8,128)}), (f32[128,1600]{1,0:T(8,128)}, f32[256,64]{1,0:T(8,128)})) %all-reduce.4.cloned.1.call-update) | async-done | bytes 884752 | tf_op jit(solution)/shard_map/psum | solution.py:153
  371.7 1.4 constant_dynamic-slice_fusion
  373.1 1.2 constant_dynamic-slice_fusion.3
  (73 shorter events, 2.2 us)
Async XLA Ops:
  7.2 4.8 %copy-start = (bf16[2,64,1024]{2,1,0:T(8,128)(2,1)S(1)}, bf16[2,64,1024]{2,1,0:T(8,128)(2,1)}, u32[]{:S(2)}) copy-start(bf16[2,64,1024]{2,1,0:T(8,128)(2,1)} %param.11) | copy-start | bytes 786436
  7.2 6.0 %copy-start.10 = (bf16[1,2,64,4096]{3,2,1,0:T(8,128)(2,1)S(1)}, bf16[1,2,64,4096]{3,2,1,0:T(8,128)(2,1)}, u32[]{:S(2)}) copy-start(bf16[1,2,64,4096]{3,2,1,0:T(8,128)(2,1)} %param.10) | copy-start | bytes 3145732
  7.2 364.5 %all-reduce.4.cloned.1.call-start = ((), (), s32[]{:S(2)}) async-start(), calls=%async_computation | async-start | bytes 1966080 | tf_op jit(solution)/shard_map/psum | solution.py:153
  7.2 66.5 %collective-permute-start = (bf16[2,1024]{1,0:T(2,128)(2,1)}, bf16[2,1024]{1,0:T(2,128)(2,1)S(1)}, u32[]{:S(2)}, u32[]{:S(2)}) collective-permute-start(bf16[2,1024]{1,0:T(2,128)(2,1)} %bitcast.87), channel_id=1, source_target_pairs={{0,2},{2,0},{4,6},{6,4},{8,10},{10,8},{12,14},{14,12},{16,18},{18,... | collective-permute-start | bytes 12296 | tf_op jit(solution)/shard_map/ppermute | solution.py:9
  24.5 7.0 %copy-start.15 = (f32[256,64]{0,1:T(8,128)S(1)}, f32[256,64]{0,1:T(8,128)}, u32[]{:S(2)}) copy-start(f32[256,64]{0,1:T(8,128)} %param.13) | copy-start | bytes 196612
  24.5 7.2 %copy-start.11 = (bf16[64,64,4,4]{1,0,3,2:T(8,128)(2,1)S(1)}, bf16[64,64,4,4]{1,0,3,2:T(8,128)(2,1)}, u32[]{:S(2)}) copy-start(bf16[64,64,4,4]{1,0,3,2:T(8,128)(2,1)} %copy.169) | copy-start | bytes 393220
  24.5 7.2 %copy-start.17 = (pred[16,5]{0,1:T(8,128)(4,1)S(1)}, pred[16,5]{0,1:T(8,128)(4,1)}, u32[]{:S(2)}) copy-start(pred[16,5]{0,1:T(8,128)(4,1)} %constant.131) | copy-start | bytes 244
  36.4 2.8 copy-start.8
  36.5 1.1 copy-start.13
  40.5 39.9 %collective-permute-start.1 = (bf16[2,64,1024]{1,2,0:T(8,128)(2,1)}, bf16[2,64,1024]{1,2,0:T(8,128)(2,1)}, u32[]{:S(2)}, u32[]{:S(2)}) collective-permute-start(bf16[2,64,1024]{1,2,0:T(8,128)(2,1)} %bitcast.12), channel_id=1, source_target_pairs={{0,2},{2,0},{4,6},{6,4},{8,10},{10,8},{12,14},{14,12},{16,18},{18,... | collective-permute-start | bytes 786440 | tf_op jit(solution)/shard_map/ppermute | solution.py:9
  42.8 3.6 copy-start.21
  42.8 4.8 %copy-start.18 = (s32[64,4]{0,1:T(4,128)S(1)}, s32[64,4]{0,1:T(4,128)}, u32[]{:S(2)}) copy-start(s32[64,4]{0,1:T(4,128)} %param.15) | copy-start | bytes 3076
  53.4 1.6 copy-start.2
  55.1 2.3 copy-start.16
  66.0 4.8 %copy-start.3 = (bf16[64,64,2,8,10]{1,0,4,3,2:T(8,128)(2,1)S(1)}, bf16[64,64,2,8,10]{1,0,4,3,2:T(8,128)(2,1)}, u32[]{:S(2)}) copy-start(bf16[64,64,2,8,10]{1,0,4,3,2:T(8,128)(2,1)} %fusion.17) | copy-start | bytes 3932164
  96.1 1.3 copy-start.9
  96.1 1.3 copy-start.14
  97.4 2.2 copy-start.5
  97.4 2.5 copy-start.6
  97.4 3.3 copy-start.7
  98.9 2.8 copy-start.4
  101.7 5.5 %copy-start.19 = (pred[256]{0:T(512)(128)(4,1)S(1)}, pred[256]{0:T(512)(128)(4,1)}, u32[]{:S(2)}) copy-start(pred[256]{0:T(512)(128)(4,1)} %iota_compare_fusion.9) | copy-start | bytes 772
  106.7 1.5 copy-start.20
  108.0 1.3 copy-start.12
  113.0 261.3 %copy-start.1 = (bf16[2,64,1024]{2,1,0:T(8,128)(2,1)S(1)}, bf16[2,64,1024]{2,1,0:T(8,128)(2,1)}, u32[]{:S(2)}) copy-start(bf16[2,64,1024]{2,1,0:T(8,128)(2,1)} %param.11) | copy-start | bytes 786436
Sparse Core Ops, SparseCore 0:
  109.5 262.1 all-reduce.3
where the time goes:
time: 382 us; the launch traced here: 381 us
  waiting for transfers between devices  252 us (66%)
  local copies, waits for them, and re-layouts  63.1 us (17%)
  matrix products  19.1 us (5%)
  between operations  17.1 us (4%)
  blocking collectives  15.2 us (4%)
  other arithmetic  14.5 us (4%)
    psum x1, waiting for transfers between devices, local(): summed = lax.psum(weight_term, ('scene', 'tile'))  252 us
    another operation x9, local copies, waits for them, and re-layouts, local(): feature_grid = features.reshape(patches, channels, grid_side, grid_side)  26 us
    conv_general_dilated x6, matrix products, apply_convolution(): lax.conv_general_dilated(left_operand, right_operand, window_strides, bor...  19.1 us
    all_gather x1, blocking collectives, local(): lax.all_gather(swapped_out, 'tile', axis=0, tiled=True)  9.36 us
    unnamed x49, local copies, waits for them, and re-layouts  8.82 us
  transfers between devices with their start and end apart: 3, of which 1 were waited for; matrix products, arithmetic and copies ran while one was open for 19% of the time, Pallas kernels for 0%

commit v1 on v0

--- a/solution.py
+++ b/solution.py
@@ -3,6 +3,19 @@
 import jax.numpy as jnp
 from jax import lax
 from jax.sharding import PartitionSpec as P
+
+
+def get_the_steps_all(target, named_axis="tile"):
+    next_value = jnp.concatenate(
+        lax.all_to_all(
+            jnp.stack([target for _ in range(lax.axis_size(named_axis))]),
+            split_axis=0,
+            axis_name=named_axis,
+            concat_axis=0,
+        ),
+        0,
+    )
+    return next_value
 
 
 def from_partner(x, axis, distance):
@@ -92,7 +105,7 @@
     first_patch = tile_index * patches
     swapped_out, swapped_cot = from_partner((branch_out, own_cotangent), "scene", 0)
     partner_out, partner_cot = (
-        lax.all_gather(swapped_out, "tile", axis=0, tiled=True),
+        get_the_steps_all(swapped_out),
         lax.all_gather(swapped_cot, "tile", axis=0, tiled=True),
     )
     matched = match_rows(pairing_row, branch, first_patch, patches)

time: 382 us -> 382 us (level)
  blocking collectives: 15.2 us -> 5.85 us
  starting transfers between devices: 0.51 us -> 4.75 us
    all_gather x1 -> x0, blocking collectives: 9.36 us -> none  [local(): lax.all_gather(swapped_out, 'tile', axis=0, tiled=True)]
    all_to_all x0 -> x1, starting transfers between devices: none -> 4.22 us  [get_the_steps_all(): lax.all_to_all(jnp.stack([target for _ in range(lax.axis_size(named_axis)...]
  transfers between devices with their start and end apart: 3 -> 4, of which waited for: 1 -> 1; matrix products, arithmetic and copies ran while one was open for 19% -> 20% of each run, Pallas kernels for 0% -> 0%
where the time goes in v1:
time: 382 us
  waiting for transfers between devices  253 us (66%)
  local copies, waits for them, and re-layouts  65.3 us (17%)
  matrix products  19.1 us (5%)
  between operations  17.2 us (5%)
  other arithmetic  16.8 us (4%)
  blocking collectives  5.85 us (2%)
  starting transfers between devices  4.75 us (1%)
    psum x1, waiting for transfers between devices, local(): summed = lax.psum(weight_term, ('scene', 'tile'))  253 us
    another operation x9, local copies, waits for them, and re-layouts, local(): feature_grid = features.reshape(patches, channels, grid_side, grid_side)  26.1 us
    conv_general_dilated x6, matrix products, apply_convolution(): lax.conv_general_dilated(left_operand, right_operand, window_strides, bor...  19.1 us
    unnamed x49, local copies, waits for them, and re-layouts  8.82 us
  transfers between devices with their start and end apart: 4, of which 1 were waited for; matrix products, arithmetic and copies ran while one was open for 20% of the time, Pallas kernels for 0%

profile of v1, /device:TPU:2, one launch (start us, length us, event | category | flops | bytes accessed | tf_op | source)
XLA Modules:
  0.0 381.6 jit_solution(12697085395429368156)
XLA Ops:
  7.3 1.3 dynamic_slice.30
  9.9 0.9 constant_dynamic-slice_fusion.1
  11.1 0.8 copy.171
  12.1 1.0 copy.169
  13.1 2.3 reshape_squeeze.3
  15.4 2.9 copy.200
  18.3 3.4 fusion.59
  21.7 2.7 fusion.12
  24.4 6.3 %copy.167 = bf16[64,64,2,8,13]{0,3,2,4,1:T(8,128)(2,1)} copy(bf16[64,64,2,8,13]{1,0,4,3,2:T(8,128)(2,1)} %fusion.12) | data formatting | bytes 3407872 | tf_op jit(solution)/shard_map/conv_general_dilated | solution.py:34
  31.3 0.2 dynamic-slice_reduce_fusion
  31.5 4.8 %fusion.27 = f32[32,16,5,64]{3,1,2,0:T(8,128)S(1)} fusion(bf16[64,64,4,4]{1,0,3,2:T(8,128)(2,1)S(1)} %copy-done.11, bf16[64,64,2,8,13]{0,3,2,4,1:T(8,128)(2,1)} %copy.167, f32[64]{0:T(128)S(1)} %dynamic-slice_reduce_fusion, pred[16,5]{0,1:T(8,128)(4,1)S(1)} %copy-done.17), kind=kOutput, calls=%fused_computation.39 | convolution fusion | flops 330629120 | bytes 2490704 | tf_op jit(solution)/shard_map/conv_general_dilated | solution.py:34
  36.4 0.5 select_bitcast_fusion
  36.9 0.5 copy-done.13
  37.4 1.7 convolution_convert_fusion.1
  39.3 1.0 copy.173
  40.3 0.4 collective-permute-start.1
  40.7 0.8 fusion.58
  41.6 3.6 fusion.57
  45.2 0.6 dynamic_slice.28
  46.4 0.2 dynamic-slice_reduce_fusion.1
  46.7 0.6 gather_fusion.2
  47.4 0.6 gather_fusion.3
  48.0 4.2 %fusion.15 = (bf16[64,64,2,8,10]{1,0,4,3,2:T(8,128)(2,1)}, bf16[64,64,2,8,10]{1,0,4,3,2:T(8,128)(2,1)S(1)}) fusion(bf16[64,64,2,7,1]{1,0,4,3,2:T(8,128)(2,1)} %get-tuple-element.12, bf16[64,64,2,8,9]{1,0,4,3,2:T(8,128)(2,1)} %get-tuple-element.10, bf16[64,64,2,7,1]{1,0,4,3,2:T(8,128)(2,1)} %get-tuple-element.14, bf16[64,64,2,8,9]{1,0,4,3,2:T(8,128)(2,1)} %get-tuple-element.11), kind=kLoop, calls=%fused_computation.22 | loop fusion | flops 7864320 | bytes 5210112 | tf_op jit(solution)/shard_map/reshape;squeeze | solution.py:92
  52.3 0.7 slice.38
  53.0 0.9 copy-done.2
  53.9 1.2 iota_compare_fusion.9
  55.0 2.2 fusion.17
  57.3 2.4 pad_maximum_fusion
  59.7 2.3 copy.174
  62.0 4.2 %all-to-all-start = ((bf16[2,2,64,1024]{3,2,1,0:T(8,128)(2,1)}), bf16[2,2,64,1024]{3,2,1,0:T(8,128)(2,1)}, u32[]{:S(2)}, u32[]{:S(2)}) async-start(bf16[2,2,64,1024]{3,2,1,0:T(8,128)(2,1)} %copy.174), calls=%async_computation | async-start | bytes 1048576 | tf_op jit(solution)/shard_map/all_to_all | solution.py:10
  66.4 4.7 %copy.187 = bf16[64,64,2,8,10]{0,3,2,4,1:T(8,128)(2,1)} copy(bf16[64,64,2,8,10]{1,0,4,3,2:T(8,128)(2,1)} %copy-done.2) | data formatting | bytes 2621440 | tf_op jit(solution)/shard_map/reshape;squeeze | solution.py:92
  71.1 0.6 broadcast_in_dim.101
  72.0 3.0 copy.189
  74.9 4.8 %copy.185 = bf16[64,64,2,8,10]{0,3,2,4,1:T(8,128)(2,1)} copy(bf16[64,64,2,8,10]{1,0,4,3,2:T(8,128)(2,1)} %get-tuple-element.23) | data formatting | bytes 2621440 | tf_op jit(solution)/shard_map/reshape;squeeze | solution.py:92
  79.7 2.9 copy.188
  82.6 5.9 %all-gather = bf16[2,2,1024]{2,1,0:T(2,128)(2,1)S(1)} all-gather(bf16[1,2,1024]{2,1,0:T(2,128)(2,1)S(1)} %bitcast.90), channel_id=1, replica_groups=mesh['scene'=128,'tile'=2] {'tile'}, dimensions={0}, use_global_device_ids=true | all-gather | bytes 12288 | tf_op jit(solution)/shard_map/all_gather | solution.py:109
  88.5 0.6 gather_fusion
  89.3 1.6 gather_fusion.1
  90.9 0.3 copy.175
  91.1 0.3 fusion.66
  91.5 0.3 multiply_convert_fusion.1
  91.8 0.2 copy.201
  92.1 3.1 fusion.49
  95.1 0.2 copy.195
  95.8 0.2 fusion.30
  96.1 0.7 copy-done.9
  96.8 1.5 convert_select_fusion
  98.3 0.4 select_reduce_fusion
  99.0 0.4 copy-done.6
  99.4 0.8 copy-done.7
  100.1 1.0 copy-done.4
  101.1 5.0 %fusion = f32[64,64,4,4,1]{0,1,3,4,2:T(8,128)S(1)} fusion(bf16[64,64,16,10,1]{0,2,4,3,1:T(8,128)(2,1)S(1)} %bitcast.83, bf16[64,64,16,10,1]{0,2,4,3,1:T(8,128)(2,1)S(1)} %bitcast.81, bf16[64,64,16,10,1]{0,2,4,3,1:T(8,128)(2,1)S(1)} %copy-done.5, bf16[64,64,16,10,1]{0,2,4,3,1:T(8,128)(2,1)S(1)} %bitcast.82, bf16[32,16,5,64]{3,1,2,0:T(8,128)(2,1)S(1)} %get-tuple-element.21), kind=kOutput, calls=%fused_computation.4 | convolution fusion | flops 351272960 | bytes 5832704 | tf_op jit(solution)/shard_map/conv_general_dilated | solution.py:34
  106.1 0.3 copy.191
  106.5 0.2 copy.196
  106.7 0.7 broadcast_select_fusion
  107.4 0.2 fusion.43
  107.7 1.1 bitcast_select_fusion
  108.8 3.1 convolution_convert_fusion
  111.9 0.5 copy.182
  112.4 2.9 copy.183
  115.4 4.1 %broadcast_in_dim_reshape.3 = bf16[1,2,64,4096]{3,2,1,0:T(8,128)(2,1)} reshape(bf16[2,64,64,64]{3,2,1,0:T(8,128)(2,1)} %copy.183) | data formatting | bytes 2097152 | tf_op jit(solution)/shard_map/broadcast_in_dim;reshape | solution.py:179
  119.5 252.7 %all-reduce.4.cloned.1.call-done = (f32[128,1600]{1,0:T(8,128)}, f32[256,64]{1,0:T(8,128)}) async-done(((f32[128,1600]{1,0:T(8,128)}, f32[256,64]{1,0:T(8,128)}), (f32[128,1600]{1,0:T(8,128)}, f32[256,64]{1,0:T(8,128)})) %all-reduce.4.cloned.1.call-update) | async-done | bytes 884752 | tf_op jit(solution)/shard_map/psum | solution.py:166
  372.2 1.4 constant_dynamic-slice_fusion
  373.6 1.2 constant_dynamic-slice_fusion.3
  (75 shorter events, 2.4 us)
Async XLA Ops:
  7.2 4.7 %copy-start = (bf16[2,64,1024]{2,1,0:T(8,128)(2,1)S(1)}, bf16[2,64,1024]{2,1,0:T(8,128)(2,1)}, u32[]{:S(2)}) copy-start(bf16[2,64,1024]{2,1,0:T(8,128)(2,1)} %param.11) | copy-start | bytes 786436
  7.2 5.9 %copy-start.10 = (bf16[1,2,64,4096]{3,2,1,0:T(8,128)(2,1)S(1)}, bf16[1,2,64,4096]{3,2,1,0:T(8,128)(2,1)}, u32[]{:S(2)}) copy-start(bf16[1,2,64,4096]{3,2,1,0:T(8,128)(2,1)} %param.10) | copy-start | bytes 3145732
  7.2 75.5 %collective-permute-start = (bf16[2,1024]{1,0:T(2,128)(2,1)}, bf16[2,1024]{1,0:T(2,128)(2,1)S(1)}, u32[]{:S(2)}, u32[]{:S(2)}) collective-permute-start(bf16[2,1024]{1,0:T(2,128)(2,1)} %bitcast.89), channel_id=1, source_target_pairs={{0,2},{2,0},{4,6},{6,4},{8,10},{10,8},{12,14},{14,12},{16,18},{18,... | collective-permute-start | bytes 12296 | tf_op jit(solution)/shard_map/ppermute | solution.py:22
  24.4 6.9 %copy-start.15 = (f32[256,64]{0,1:T(8,128)S(1)}, f32[256,64]{0,1:T(8,128)}, u32[]{:S(2)}) copy-start(f32[256,64]{0,1:T(8,128)} %param.13) | copy-start | bytes 196612
  24.4 7.1 %copy-start.11 = (bf16[64,64,4,4]{1,0,3,2:T(8,128)(2,1)S(1)}, bf16[64,64,4,4]{1,0,3,2:T(8,128)(2,1)}, u32[]{:S(2)}) copy-start(bf16[64,64,4,4]{1,0,3,2:T(8,128)(2,1)} %copy.169) | copy-start | bytes 393220
  24.4 7.1 %copy-start.17 = (pred[16,5]{0,1:T(8,128)(4,1)S(1)}, pred[16,5]{0,1:T(8,128)(4,1)}, u32[]{:S(2)}) copy-start(pred[16,5]{0,1:T(8,128)(4,1)} %constant.131) | copy-start | bytes 244
  36.3 2.8 copy-start.8
  36.3 1.1 copy-start.13
  40.3 16.9 %collective-permute-start.1 = (bf16[2,64,1024]{1,2,0:T(8,128)(2,1)}, bf16[2,64,1024]{1,2,0:T(8,128)(2,1)}, u32[]{:S(2)}, u32[]{:S(2)}) collective-permute-start(bf16[2,64,1024]{1,2,0:T(8,128)(2,1)} %bitcast.12), channel_id=1, source_target_pairs={{0,2},{2,0},{4,6},{6,4},{8,10},{10,8},{12,14},{14,12},{16,18},{18,... | collective-permute-start | bytes 786440 | tf_op jit(solution)/shard_map/ppermute | solution.py:22
  41.6 3.6 copy-start.21
  41.6 4.9 %copy-start.18 = (s32[64,4]{0,1:T(4,128)S(1)}, s32[64,4]{0,1:T(4,128)}, u32[]{:S(2)}) copy-start(s32[64,4]{0,1:T(4,128)} %param.15) | copy-start | bytes 3076
  52.3 1.6 copy-start.2
  57.3 9.1 %copy-start.16 = (bf16[1,2,1024]{2,1,0:T(2,128)(2,1)S(1)}, bf16[1,2,1024]{2,1,0:T(2,128)(2,1)}, u32[]{:S(2)}) copy-start(bf16[1,2,1024]{2,1,0:T(2,128)(2,1)} %param.14) | copy-start | bytes 12292
  62.0 27.2 %all-to-all-start = ((bf16[2,2,64,1024]{3,2,1,0:T(8,128)(2,1)}), bf16[2,2,64,1024]{3,2,1,0:T(8,128)(2,1)}, u32[]{:S(2)}, u32[]{:S(2)}) async-start(bf16[2,2,64,1024]{3,2,1,0:T(8,128)(2,1)} %copy.174), calls=%async_computation | async-start | bytes 1048576 | tf_op jit(solution)/shard_map/all_to_all | solution.py:10
  66.2 305.9 %all-reduce.4.cloned.1.call-start = ((), (), s32[]{:S(2)}) async-start(), calls=%async_computation.1 | async-start | bytes 1966080 | tf_op jit(solution)/shard_map/psum | solution.py:166
  74.9 4.8 %copy-start.3 = (bf16[64,64,2,8,10]{1,0,4,3,2:T(8,128)(2,1)S(1)}, bf16[64,64,2,8,10]{1,0,4,3,2:T(8,128)(2,1)}, u32[]{:S(2)}) copy-start(bf16[64,64,2,8,10]{1,0,4,3,2:T(8,128)(2,1)} %fusion.17) | copy-start | bytes 3932164
  95.5 1.3 copy-start.9
  95.5 1.3 copy-start.14
  96.8 2.2 copy-start.5
  96.8 2.5 copy-start.6
  96.8 3.3 copy-start.7
  98.3 2.8 copy-start.4
  101.1 5.5 %copy-start.19 = (pred[256]{0:T(512)(128)(4,1)S(1)}, pred[256]{0:T(512)(128)(4,1)}, u32[]{:S(2)}) copy-start(pred[256]{0:T(512)(128)(4,1)} %iota_compare_fusion.9) | copy-start | bytes 772
  106.1 1.6 copy-start.20
  107.4 1.3 copy-start.12
  112.4 262.4 %copy-start.1 = (bf16[2,64,1024]{2,1,0:T(8,128)(2,1)S(1)}, bf16[2,64,1024]{2,1,0:T(8,128)(2,1)}, u32[]{:S(2)}) copy-start(bf16[2,64,1024]{2,1,0:T(8,128)(2,1)} %param.11) | copy-start | bytes 786436
Sparse Core Ops, SparseCore 0:
  108.9 263.2 all-reduce.3
